TPU v7x, 512 devices: a whole 4x8x8 slice. The times are simulated.
512 devices in a mesh: scen: 8 (over y), blk: 64 (over z, x, core).
Axes of the slice: x: 4, y: 8, z: 8, core: 2. Of those that a mesh axis runs over, the one named last changes fastest.
Arguments:
- returns: bfloat16 [512, 32768], P(('scen', 'blk')), may hold values from -6 to 6
- vol_hist: float32 [512, 32768], P(('scen', 'blk')), may hold values from 0.5 to 5.5, as said below
- vol_now: float32 [32768], replicated, may hold values from 0.5 to 2
- sensitivity: bfloat16 [16384, 128, 128], P('blk'), may hold values from -0.109375 to 0.109375
- block_pairs: int32 [16384, 3], P('blk'), may hold values from 0 to 255, as said below
- book_order: int32 [128], replicated, may hold values from 0 to 127, each once
Outputs:
- profit_loss: float32 [512, 16384], P('scen', 'blk')
- book_rms: float32 [16384], P('blk')
Inputs may be any that keep to these rules, and one draw needn't show every extreme that they name: `block_pairs`: each index k of blk holds 256 slots; their factor blocks lie in k * 4 to k * 4 + 3; on each index the live slots come first; some index has all 256 slots live. `vol_hist`: positive volatilities.
All inputs are finite; a program needn't handle non-finite values.
Results may differ from a plain program's by a relative error of at most 0.0029.
Values may be sent and summed in bfloat16 or wider, within the bound.
A program may use at most 64 MiB of HBM per device.

v0:
```python
import jax
import jax.numpy as jnp
from jax import lax
from jax.sharding import PartitionSpec as P


def shards(returns, vol_hist, vol_now, sensitivity, block_pairs, book_order):
    rescaled = (returns.astype(jnp.float32) * vol_now[None, :] / vol_hist).astype(jnp.bfloat16)
    groups = lax.axis_size("blk")
    column = lax.axis_index("blk")
    block_size = sensitivity.shape[1]
    own_width = rescaled.shape[1] // groups
    gathered = lax.all_gather(rescaled, "blk", axis=0, tiled=True)
    own_shocks = lax.dynamic_slice_in_dim(gathered, column * own_width, own_width, 1)
    scen_rows = own_shocks.shape[0]
    local_blocks = own_shocks.reshape(scen_rows, own_width // block_size, block_size)
    factor_local = block_pairs[:, 0] - column * (own_width // block_size)
    picked = jnp.take(local_blocks, factor_local, axis=1)
    products = jnp.einsum("skc,kcd->ksd", picked, sensitivity, preferred_element_type=jnp.float32)
    book_blocks = book_order.shape[0]
    matches = book_order[None, :] == block_pairs[:, 1][:, None]
    position = jnp.sum(
        jnp.where(matches, jnp.arange(book_blocks, dtype=jnp.int32)[None, :], 0), axis=1
    )
    live_weight = block_pairs[:, 2].astype(jnp.float32)
    selector = jnp.where(
        jnp.arange(book_blocks, dtype=jnp.int32)[:, None] == position[None, :],
        live_weight[None, :],
        0.0,
    )
    partial_sum = jnp.einsum("bk,ksd->bsd", selector, products, precision=lax.Precision.HIGHEST)
    owned_books = lax.psum_scatter(partial_sum, "blk", scatter_dimension=0, tiled=True)
    profit_loss = owned_books.transpose(1, 0, 2).reshape(scen_rows, -1)
    squares = lax.psum(jnp.sum(profit_loss * profit_loss, axis=0), "scen")
    total_rows = scen_rows * lax.axis_size("scen")
    book_rms = jnp.sqrt(squares / total_rows + 1e-06)
    return (profit_loss, book_rms)


def solution(mesh):
    return jax.shard_map(
        shards,
        mesh=mesh,
        in_specs=(
            P(("scen", "blk"), None),
            P(("scen", "blk"), None),
            P(),
            P("blk", None, None),
            P("blk", None),
            P(),
        ),
        out_specs=(P("scen", "blk"), P("blk")),
        check_vma=False,
    )
```

profile of v0, /device:TPU:2, one launch (start us, length us, event | category | flops | bytes accessed | tf_op | source)
XLA Modules:
  0.0 306.9 jit_solution(5500297832278596794)
XLA Ops:
  7.2 0.0 all-gather.3.cloned.1.call-start
  7.2 1.9 convert_bitcast_fusion
  9.1 0.0 all-gather.3.cloned.1.call-update
  9.1 0.0 reduce-scatter.2.cloned.1.call-start
  9.2 0.7 and_reduce_fusion
  9.9 0.8 fusion.15
  10.7 0.8 select_reduce_fusion
  11.5 93.0 %all-gather.3.cloned.1.call-done = bf16[64,1,32768]{2,1,0:T(2,128)(2,1)} async-done(((bf16[1,1,32768]{2,1,0:T(2,128)(2,1)}), bf16[64,1,32768]{2,1,0:T(2,128)(2,1)}) %all-gather.3.cloned.1.call-update) | async-done | bytes 4194320 | tf_op jit(solution)/shard_map/all_gather | solution.py:13
  104.5 1.3 dynamic-slice_reduce_fusion
  105.8 3.0 gather_fusion
  108.8 7.0 %fusion.2 = f32[256,64,128]{2,1,0:T(8,128)S(1)} fusion(bf16[256,128,128]{2,1,0:T(8,128)(2,1)} %param.9, bf16[256,64,128]{2,1,0:T(8,128)(2,1)} %gather_fusion, pred[256]{0:T(512)(128)(4,1)S(1)} %get-tuple-element.2), kind=kOutput, calls=%fused_computation.3 | convolution fusion | flops 538968064 | bytes 20971776 | tf_op jit(solution)/shard_map/skc,kcd->ksd/dot_general | solution.py:19
  115.9 10.2 %fusion = f32[128,64,128]{2,0,1:T(8,128)S(1)} fusion(f32[256,64,128]{2,1,0:T(8,128)S(1)} %fusion.2, f32[256]{0:T(256)S(1)} %bitcast.32, s32[256]{0:T(256)S(1)} %select_reduce_fusion), kind=kOutput, calls=%fused_computation.1 | convolution fusion | flops 3221291008 | bytes 12584960 | tf_op jit(solution)/shard_map/bk,ksd->bsd/dot_general | solution.py:31
  126.1 4.4 %copy.18 = f32[128,64,128]{2,1,0:T(8,128)} copy(f32[128,64,128]{2,0,1:T(8,128)S(1)} %fusion) | data formatting | bytes 8388608 | tf_op jit(solution)/shard_map/bk,ksd->bsd/dot_general | solution.py:31
  130.4 0.0 reduce-scatter.2.cloned.1.call-update
  130.5 149.7 %reduce-scatter.2.cloned.1.call-done = f32[2,64,128]{2,1,0:T(8,128)} async-done(((f32[128,64,128]{2,1,0:T(8,128)}), f32[2,64,128]{2,1,0:T(8,128)}) %reduce-scatter.2.cloned.1.call-update) | async-done | bytes 65552 | tf_op jit(solution)/shard_map/reduce_scatter | solution.py:32
  280.2 0.9 fusion.9
  281.1 17.0 %psum.7 = f32[256]{0:T(256)S(1)} all-reduce(f32[256]{0:T(256)S(1)} %bitcast.29), channel_id=1, replica_groups=mesh['scen'=8,'blk'=64] {'scen'}, use_global_device_ids=true, to_apply=%region_3.4 | all-reduce | flops 256 | bytes 2048 | tf_op jit(solution)/shard_map/psum | solution.py:34
  298.0 0.6 add_sqrt_fusion
  298.6 1.5 copy_bitcast_fusion
  (2 shorter events, 0.0 us)
Async XLA Ops:
  7.2 97.4 %all-gather.3.cloned.1.call-start = ((), (), s32[]{:S(2)}) async-start(), calls=%async_computation.2 | async-start | bytes 8519680 | tf_op jit(solution)/shard_map/all_gather | solution.py:13
  9.1 271.0 %reduce-scatter.2.cloned.1.call-start = ((), (), s32[]{:S(2)}) async-start(), calls=%async_computation.1 | async-start | bytes 4259840 | tf_op jit(solution)/shard_map/reduce_scatter | solution.py:32
Sparse Core Ops, SparseCore 0:
  11.3 93.1 all-gather.2
  130.6 149.5 reduce-scatter.1
where the time goes:
time: 307 us
  waiting for transfers between devices  243 us (79%)
  matrix products  17.2 us (6%)
  blocking collectives  17 us (6%)
  between operations  14.1 us (5%)
  local copies, waits for them, and re-layouts  10.1 us (3%)
  other arithmetic  5.67 us (2%)
    reduce_scatter x1, waiting for transfers between devices, shards(): lax.psum_scatter(partial_sum, 'blk', scatter_dimension=0, tiled=True)  150 us
    all_gather x1, waiting for transfers between devices, shards(): gathered = lax.all_gather(rescaled, 'blk', axis=0, tiled=True)  93 us
    psum x1, blocking collectives, shards(): squares = lax.psum(jnp.sum(profit_loss * profit_loss, axis=0), 'scen')  17 us
    dot_general x1, matrix products, shards(): jnp.einsum('bk,ksd->bsd', selector, products, precision=lax.Precision.HIG...  10.2 us
    dot_general x1, matrix products, shards(): jnp.einsum('skc,kcd->ksd', picked, sensitivity, preferred_element_type=jn...  7.02 us
  transfers between devices with their start and end apart: 2, of which 2 were waited for; matrix products, arithmetic and copies ran while one was open for 1% of the time, Pallas kernels for 0%

commit v1 on v0

--- a/solution.py
+++ b/solution.py
@@ -10,7 +10,9 @@
     column = lax.axis_index("blk")
     block_size = sensitivity.shape[1]
     own_width = rescaled.shape[1] // groups
-    gathered = lax.all_gather(rescaled, "blk", axis=0, tiled=True)
+    gathered = jnp.concatenate(
+        lax.all_to_all(jnp.stack([rescaled] * lax.axis_size("blk")), "blk", 0, 0), axis=0
+    )
     own_shocks = lax.dynamic_slice_in_dim(gathered, column * own_width, own_width, 1)
     scen_rows = own_shocks.shape[0]
     local_blocks = own_shocks.reshape(scen_rows, own_width // block_size, block_size)

time: 307 us -> 382 us (1.24)
  local copies, waits for them, and re-layouts: 10.1 us -> 43.9 us
  other arithmetic: 5.67 us -> 29.9 us
  starting transfers between devices: 0.08 us -> 14.2 us
    all_to_all x0 -> x1, waiting for transfers between devices: none -> 95.8 us  [shards(): lax.all_to_all(jnp.stack([rescaled] * lax.axis_size('blk')), 'blk', 0, 0)]
    all_gather x1 -> x0, waiting for transfers between devices: 93 us -> none  [shards(): gathered = lax.all_gather(rescaled, 'blk', axis=0, tiled=True)]
    unnamed x0 -> x6, local copies, waits for them, and re-layouts: none -> 27.6 us
    another operation x0 -> x1, other arithmetic: none -> 26.7 us  [shards(): jnp.stack([rescaled] * lax.axis_size('blk'))]
    all_to_all x0 -> x1, starting transfers between devices: none -> 14.2 us  [shards(): lax.all_to_all(jnp.stack([rescaled] * lax.axis_size('blk')), 'blk', 0, 0)]
    another operation x0 -> x2, local copies, waits for them, and re-layouts: none -> 6.13 us  [shards(): jnp.stack([rescaled] * lax.axis_size('blk'))]
  transfers between devices with their start and end apart: 2 -> 2, of which waited for: 2 -> 2; matrix products, arithmetic and copies ran while one was open for 1% -> 0% of each run, Pallas kernels for 0% -> 0%
where the time goes in v1:
time: 382 us; the launch traced here: 381 us
  waiting for transfers between devices  244 us (64%)
  local copies, waits for them, and re-layouts  43.9 us (11%)
  other arithmetic  29.9 us (8%)
  matrix products  17.3 us (5%)
  blocking collectives  16.9 us (4%)
  starting transfers between devices  14.2 us (4%)
  between operations  14.1 us (4%)
    reduce_scatter x1, waiting for transfers between devices, shards(): lax.psum_scatter(partial_sum, 'blk', scatter_dimension=0, tiled=True)  148 us
    all_to_all x1, waiting for transfers between devices, shards(): lax.all_to_all(jnp.stack([rescaled] * lax.axis_size('blk')), 'blk', 0, 0)  95.8 us
    unnamed x6, local copies, waits for them, and re-layouts  27.6 us
    another operation x1, other arithmetic, shards(): jnp.stack([rescaled] * lax.axis_size('blk'))  26.7 us
    psum x1, blocking collectives, shards(): squares = lax.psum(jnp.sum(profit_loss * profit_loss, axis=0), 'scen')  16.9 us
    all_to_all x1, starting transfers between devices, shards(): lax.all_to_all(jnp.stack([rescaled] * lax.axis_size('blk')), 'blk', 0, 0)  14.2 us
    dot_general x1, matrix products, shards(): jnp.einsum('bk,ksd->bsd', selector, products, precision=lax.Precision.HIG...  10.3 us
  transfers between devices with their start and end apart: 2, of which 2 were waited for; matrix products, arithmetic and copies ran while one was open for 0% of the time, Pallas kernels for 0%

profile of v1, /device:TPU:2, one launch (start us, length us, event | category | flops | bytes accessed | tf_op | source)
XLA Modules:
  0.0 380.6 jit_solution(13877792165904643910)
XLA Ops:
  7.2 1.5 convert_reduce_fusion
  8.7 5.6 %stack.2 = bf16[64,1,32768]{2,1,0:T(2,128)(2,1)} broadcast(bf16[32768]{0:T(1024)(128)(2,1)S(1)} %convert_reduce_fusion), dimensions={2} | broadcast | bytes 4259840 | tf_op jit(solution)/shard_map/stack | solution.py:14
  14.3 0.5 broadcast.34
  14.8 26.7 %reduce.7 = bf16[64,32768]{1,0:T(8,128)(2,1)} reduce(bf16[64,1,32768]{2,1,0:T(2,128)(2,1)} %stack.2, bf16[]{:T(256)} %broadcast.34), dimensions={1}, to_apply=%stack.2.reduce_sub_computation | reduce | bytes 8388610 | tf_op jit(solution)/shard_map/stack | solution.py:14
  41.5 7.8 %reshape.43 = bf16[64,2,16384]{2,1,0:T(2,128)(2,1)} reshape(bf16[64,32768]{1,0:T(8,128)(2,1)} %reduce.7) | data formatting | bytes 8388608
  49.3 0.0 copy-start
  49.3 14.2 %all-to-all-start = ((bf16[64,2,16384]{2,1,0:T(2,128)(2,1)}), bf16[64,2,16384]{2,1,0:T(2,128)(2,1)}, u32[]{:S(2)}, u32[]{:S(2)}) async-start(bf16[64,2,16384]{2,1,0:T(2,128)(2,1)} %reshape.43), calls=%async_computation | async-start | bytes 8388608 | tf_op jit(solution)/shard_map/all_to_all | solution.py:14
  63.5 0.0 reduce-scatter.2.cloned.1.call-start
  63.6 0.0 copy-done
  63.6 0.0 copy-done.1
  63.6 0.2 select_reduce_fusion
  63.8 95.8 %all-to-all-done = bf16[64,2,16384]{2,1,0:T(2,128)(2,1)} async-done(((bf16[64,2,16384]{2,1,0:T(2,128)(2,1)}), bf16[64,2,16384]{2,1,0:T(2,128)(2,1)}, u32[]{:S(2)}, u32[]{:S(2)}) %all-to-all-start) | async-done | bytes 4194336 | tf_op jit(solution)/shard_map/all_to_all | solution.py:14
  159.6 19.8 %reshape.44 = bf16[64,1,32768]{2,1,0:T(2,128)(2,1)} reshape(bf16[64,2,16384]{2,1,0:T(2,128)(2,1)} %all-to-all-done) | data formatting | bytes 8388608
  179.4 1.3 dynamic-slice_reduce_fusion
  180.7 3.0 gather_fusion
  183.7 7.0 %fusion.2 = f32[256,64,128]{2,1,0:T(8,128)S(1)} fusion(bf16[256,128,128]{2,1,0:T(8,128)(2,1)} %param.9, bf16[256,64,128]{2,1,0:T(8,128)(2,1)} %gather_fusion, pred[256]{0:T(512)(128)(4,1)S(1)} %get-tuple-element.2), kind=kOutput, calls=%fused_computation.3 | convolution fusion | flops 538968064 | bytes 20971776 | tf_op jit(solution)/shard_map/skc,kcd->ksd/dot_general | solution.py:21
  190.8 10.3 %fusion = f32[128,64,128]{2,0,1:T(8,128)S(1)} fusion(f32[256,64,128]{2,1,0:T(8,128)S(1)} %fusion.2, f32[256]{0:T(256)S(1)} %bitcast.30, s32[256]{0:T(256)S(1)} %select_reduce_fusion), kind=kOutput, calls=%fused_computation.1 | convolution fusion | flops 3221291008 | bytes 12584960 | tf_op jit(solution)/shard_map/bk,ksd->bsd/dot_general | solution.py:33
  201.0 4.4 %copy.18 = f32[128,64,128]{2,1,0:T(8,128)} copy(f32[128,64,128]{2,0,1:T(8,128)S(1)} %fusion) | data formatting | bytes 8388608 | tf_op jit(solution)/shard_map/bk,ksd->bsd/dot_general | solution.py:33
  205.4 0.0 reduce-scatter.2.cloned.1.call-update
  205.4 148.5 %reduce-scatter.2.cloned.1.call-done = f32[2,64,128]{2,1,0:T(8,128)} async-done(((f32[128,64,128]{2,1,0:T(8,128)}), f32[2,64,128]{2,1,0:T(8,128)}) %reduce-scatter.2.cloned.1.call-update) | async-done | bytes 65552 | tf_op jit(solution)/shard_map/reduce_scatter | solution.py:34
  353.9 0.9 fusion.9
  354.8 16.9 %psum.7 = f32[256]{0:T(256)S(1)} all-reduce(f32[256]{0:T(256)S(1)} %bitcast.27), channel_id=1, replica_groups=mesh['scen'=8,'blk'=64] {'scen'}, use_global_device_ids=true, to_apply=%region_3.4 | all-reduce | flops 256 | bytes 2048 | tf_op jit(solution)/shard_map/psum | solution.py:36
  371.7 0.6 add_sqrt_fusion
  372.2 1.5 copy_bitcast_fusion
  (5 shorter events, 0.1 us)
Async XLA Ops:
  49.3 14.3 %copy-start = (s32[256,3]{0,1:T(4,128)S(1)}, s32[256,3]{0,1:T(4,128)}, u32[]{:S(2)}) copy-start(s32[256,3]{0,1:T(4,128)} %param.10) | copy-start | bytes 9220
  49.3 14.3 %copy-start.1 = (s32[128]{0:T(128)S(1)}, s32[128]{0:T(128)}, u32[]{:S(2)}) copy-start(s32[128]{0:T(128)} %param.11) | copy-start | bytes 1540
  49.3 110.3 %all-to-all-start = ((bf16[64,2,16384]{2,1,0:T(2,128)(2,1)}), bf16[64,2,16384]{2,1,0:T(2,128)(2,1)}, u32[]{:S(2)}, u32[]{:S(2)}) async-start(bf16[64,2,16384]{2,1,0:T(2,128)(2,1)} %reshape.43), calls=%async_computation | async-start | bytes 8388608 | tf_op jit(solution)/shard_map/all_to_all | solution.py:14
  63.5 290.4 %reduce-scatter.2.cloned.1.call-start = ((), (), s32[]{:S(2)}) async-start(), calls=%async_computation.2 | async-start | bytes 4259840 | tf_op jit(solution)/shard_map/reduce_scatter | solution.py:34
Sparse Core Ops, SparseCore 0:
  205.5 148.3 reduce-scatter.1
